TPU v7x, 256 devices: a whole 4x4x8 slice. The times are simulated.
256 devices in a mesh: gx: 8 (over y, core), gy: 32 (over x, z).
Axes of the slice: x: 4, y: 4, z: 8, core: 2. Of those that a mesh axis runs over, the one named last changes fastest.
Arguments:
- projected: bfloat16 [32, 512, 3072], P('gx', 'gy'), may hold values from -8 to 8
- residual: bfloat16 [32, 512, 1024], P('gx', 'gy'), may hold values from -6 to 6
- page_store: bfloat16 [256, 72, 128, 256], P(('gx', 'gy')), may hold values from -8 to 8
- page_table: int32 [32, 64], P('gx'), may hold values from 0 to 71, as said below
- lengths: int32 [32], P('gx'), may hold values from 1 to 8192, as said below
- persistent: bfloat16 [2, 16, 1024], replicated, may hold values from -8 to 8
- memory_rates: float32 [256, 3, 8], P(('gx', 'gy')), may hold values from 0.002 to 0.95
- memory_state: float32 [256, 128, 128], P(('gx', 'gy')), may hold values from -6 to 6
- momentum: float32 [256, 128, 128], P(('gx', 'gy')), may hold values from -2 to 2
- w_out: bfloat16 [1024, 1024], P('gy', 'gx'), may hold values from -0.1875 to 0.1875
Outputs:
- layer_out: bfloat16 [32, 512, 1024], P('gx', 'gy')
- memory_next: float32 [256, 128, 128], P(('gx', 'gy'))
- momentum_next: float32 [256, 128, 128], P(('gx', 'gy'))
Inputs may be any that keep to these rules, and one draw needn't show every extreme that they name: `page_table`: the 64 entries of a request's row are distinct slots. `lengths`: some request has exactly 8192 cached tokens.
All inputs are finite; a program needn't handle non-finite values.
Results may differ from a plain program's by a relative error of at most 0.012.
Values may be sent and summed in bfloat16 or wider, within the bound.
No kernel may reach another device: no remote copies, remote signals or barrier semaphores. Data moves between devices by JAX's collectives and lax.ppermute only.
A program may use at most 64 MiB of HBM per device.

v0:
```python
import math
import jax
import jax.numpy as jnp
from jax import lax
from jax.sharding import PartitionSpec as P

D = 1024
HEADS = 8
HD = 128
MB = 64
PAGE = 128
MAXP = 64
NB = 8
masked_score = -1e30


def for_sending(value):

    def short(part):
        return part.astype(jnp.bfloat16) if part.dtype == jnp.float32 else part

    return jax.tree.map(short, value)


def absorb(carried, scores, values):
    running, totals, summed = carried
    newest = jnp.maximum(running, jnp.max(scores, axis=1))
    factor = jnp.exp(running - newest)
    weights = jnp.exp(scores - newest[:, None])
    totals = totals * factor + jnp.sum(weights, axis=1)
    summed = summed * factor[:, None] + jnp.dot(
        weights.astype(jnp.bfloat16), values, preferred_element_type=jnp.float32
    )
    return (newest, totals, summed)


def recall(queries, keyed, valued, rates_here, memory, moment):
    keys_wide = keyed.astype(jnp.float32)
    keys_wide = keys_wide / jnp.sqrt(jnp.sum(keys_wide * keys_wide, axis=1, keepdims=True) + 1e-06)
    query_wide = queries.astype(jnp.float32)
    query_wide = query_wide / jnp.sqrt(
        jnp.sum(query_wide * query_wide, axis=1, keepdims=True) + 1e-06
    )
    values_wide = valued.astype(jnp.float32)
    pieces = []
    for block_id in range(NB):
        start_row = block_id * MB
        key_block = keys_wide[start_row : start_row + MB]
        query_block = query_wide[start_row : start_row + MB]
        value_block = values_wide[start_row : start_row + MB]
        pieces.append(jnp.dot(query_block, memory, precision=lax.Precision.HIGHEST))
        errors = jnp.dot(key_block, memory, precision=lax.Precision.HIGHEST) - value_block
        gradient = jnp.dot(key_block.T, errors, precision=lax.Precision.HIGHEST)
        moment = rates_here[0, block_id] * moment - rates_here[1, block_id] * gradient
        memory = (1.0 - rates_here[2, block_id]) * memory + moment
    return (jnp.concatenate(pieces, 0), memory, moment)


def shards(
    projected,
    residual,
    page_store,
    page_table,
    lengths,
    persistent,
    memory_rates,
    memory_state,
    momentum,
    w_out,
):
    groups, positions, triple = projected.shape
    pair_count = memory_state.shape[0]
    sectioned = (
        projected.reshape(groups, positions, 3, HEADS, HD)
        .transpose(0, 3, 1, 2, 4)
        .reshape(groups * HEADS, positions, 3 * HD)
    )
    paired = lax.all_to_all(sectioned, "gy", split_axis=0, concat_axis=1, tiled=True)
    offset = lax.axis_index("gy") * pair_count
    pages_block = math.gcd(MAXP, max(1, 512 // PAGE))
    key_span = pages_block * PAGE
    scaling = HD ** (-0.5)

    def handle(member):
        ordinal, segment, pages_here, rates_here, memory, moment = member
        within = offset + ordinal
        request = within // HEADS
        head_id = within % HEADS
        table_row = lax.dynamic_index_in_dim(page_table, request, 0, keepdims=False)
        length = lax.dynamic_index_in_dim(lengths, request, 0, keepdims=False)
        pers_keys = lax.dynamic_slice_in_dim(persistent[0], head_id * HD, HD, 1)
        pers_values = lax.dynamic_slice_in_dim(persistent[1], head_id * HD, HD, 1)
        queries = segment[:, :HD]
        keyed = segment[:, HD : 2 * HD]
        valued = segment[:, 2 * HD :]
        row_count = segment.shape[0]
        carried = (
            jnp.full((row_count,), masked_score, jnp.float32),
            jnp.zeros((row_count,), jnp.float32),
            jnp.zeros((row_count, HD), jnp.float32),
        )
        scores = jnp.dot(queries, pers_keys.T, preferred_element_type=jnp.float32) * scaling
        carried = absorb(carried, scores, pers_values)

        def visit_block(block_id, carried):
            first_page = block_id * pages_block
            fetched_pages = []
            for within_block in range(pages_block):
                slot_here = lax.dynamic_index_in_dim(
                    table_row, first_page + within_block, 0, keepdims=False
                )
                fetched_pages.append(
                    lax.dynamic_index_in_dim(pages_here, slot_here, 0, keepdims=False)
                )
            fetched = jnp.concatenate(fetched_pages, 0)
            key_pos = block_id * key_span + jnp.arange(key_span, dtype=jnp.int32)
            scores = (
                jnp.dot(queries, fetched[:, :HD].T, preferred_element_type=jnp.float32) * scaling
            )
            scores = jnp.where((key_pos < length)[None, :], scores, masked_score)
            return absorb(carried, scores, fetched[:, HD:])

        block_count = MAXP // pages_block
        carried = lax.fori_loop(0, block_count, visit_block, carried)
        places = jnp.arange(row_count, dtype=jnp.int32)
        causal = places[None, :] <= places[:, None]
        scores = jnp.dot(queries, keyed.T, preferred_element_type=jnp.float32) * scaling
        scores = jnp.where(causal, scores, masked_score)
        newest, totals, summed = absorb(carried, scores, valued)
        attended = summed / totals[:, None]
        recalled, memory, moment = recall(queries, keyed, valued, rates_here, memory, moment)
        mixed = (attended + recalled).astype(jnp.bfloat16)
        return (mixed, memory, moment)

    mixed, memory_next, momentum_next = lax.map(
        handle,
        (
            jnp.arange(pair_count, dtype=jnp.int32),
            paired,
            page_store,
            memory_rates,
            memory_state,
            momentum,
        ),
    )
    returned = jax.tree.map(
        lambda part, own: part.astype(own.dtype),
        lax.all_to_all(for_sending(mixed), "gy", split_axis=1, concat_axis=0, tiled=True),
        mixed,
    )
    tokens_here = (
        returned.reshape(groups, HEADS, positions, HD)
        .transpose(0, 2, 1, 3)
        .reshape(groups, positions, D)
    )
    wide_rows = lax.all_gather(w_out, "gx", axis=1, tiled=True)
    flattened = tokens_here.reshape(groups * positions, D)
    weight_piece = lax.all_gather(wide_rows, "gy", axis=0, tiled=True)
    taken = lax.slice_in_dim(flattened, 0, weight_piece.shape[0], axis=1)
    product = jnp.zeros((groups * positions, D), jnp.float32) + jnp.dot(
        taken, weight_piece, preferred_element_type=jnp.float32
    )
    layer_out = (
        (residual.reshape(groups * positions, D).astype(jnp.float32) + product)
        .astype(jnp.bfloat16)
        .reshape(groups, positions, D)
    )
    return (layer_out, memory_next, momentum_next)


def solution(mesh):
    in_specs = (
        P("gx", "gy", None),
        P("gx", "gy", None),
        P(("gx", "gy"), None, None, None),
        P("gx", None),
        P("gx"),
        P(),
        P(("gx", "gy"), None, None),
        P(("gx", "gy"), None, None),
        P(("gx", "gy"), None, None),
        P("gy", "gx"),
    )
    out_specs = (P("gx", "gy", None), P(("gx", "gy"), None, None), P(("gx", "gy"), None, None))
    return jax.shard_map(shards, mesh=mesh, in_specs=in_specs, out_specs=out_specs, check_vma=False)
```

profile of v0, /device:TPU:8, one launch (start us, length us, event | category | flops | bytes accessed | tf_op | source)
XLA Modules:
  0.0 270.0 jit_solution(14022602897338889470)
XLA Ops:
  7.2 1.1 copy.24
  8.6 1.1 reshape.79
  9.7 11.4 %all-to-all-start = ((bf16[32,16,384]{2,1,0:T(8,128)(2,1)}), bf16[32,16,384]{2,1,0:T(8,128)(2,1)S(1)}, u32[]{:S(2)}, u32[]{:S(2)}) async-start(bf16[32,16,384]{2,1,0:T(8,128)(2,1)} %reshape.79), calls=%async_computation | async-start | bytes 786432 | tf_op jit(solution)/shard_map/all_to_all | solution.py:78
  21.2 12.8 %all_gather.6 = bf16[32,1024]{1,0:T(8,128)(2,1)} all-gather(bf16[32,128]{1,0:T(8,128)(2,1)S(1)} %copy-done.6), channel_id=1, replica_groups=mesh['gx'=8,'gy'=32] {'gx'}, dimensions={1}, use_global_device_ids=true | all-gather | bytes 73728 | tf_op jit(solution)/shard_map/all_gather | solution.py:156
  42.2 1.5 fusion.33
  43.9 1.6 multiply_add_fusion.6
  46.2 180.2 %while.30 = (s32[]{:T(128)}, f32[512]{0:T(512)S(1)}, f32[512]{0:T(512)S(1)}, f32[512,128]{1,0:T(8,128)S(1)}, s32[]{:T(128)}, /*index=5*/s32[64]{0:T(128)S(1)}, b...) while((s32[]{:T(128)}, f32[512]{0:T(512)S(1)}, ...), condition=%wide.region_5.6_spmd, body=%wide.region_2.5_spmd.sunk | while | flops 137234464 | bytes 5146177 | solution.py:124
  54.7 1.0 dynamic-slice_bitcast_fusion.5
  66.0 1.0 dynamic-slice_bitcast_fusion.5
  77.3 1.0 dynamic-slice_bitcast_fusion.5
  88.5 1.0 dynamic-slice_bitcast_fusion.5
  99.8 1.0 dynamic-slice_bitcast_fusion.5
  111.1 1.0 dynamic-slice_bitcast_fusion.5
  122.3 1.0 dynamic-slice_bitcast_fusion.5
  133.6 1.0 dynamic-slice_bitcast_fusion.5
  144.9 1.0 dynamic-slice_bitcast_fusion.5
  156.1 1.0 dynamic-slice_bitcast_fusion.5
  167.4 1.0 dynamic-slice_bitcast_fusion.5
  178.6 1.0 dynamic-slice_bitcast_fusion.5
  189.9 1.0 dynamic-slice_bitcast_fusion.5
  201.1 1.0 dynamic-slice_bitcast_fusion.5
  212.4 1.0 dynamic-slice_bitcast_fusion.5
  227.1 1.5 multiply_add_fusion.5
  229.0 1.5 multiply_add_fusion.4
  230.9 1.6 multiply_add_fusion.3
  232.8 1.4 multiply_add_fusion.2
  234.6 1.5 multiply_add_fusion.1
  237.4 1.4 reduce.4
  239.6 9.8 %all-to-all-start.1 = ((bf16[32,2,1024]{2,1,0:T(2,128)(2,1)}), bf16[32,2,1024]{2,1,0:T(2,128)(2,1)S(1)}, u32[]{:S(2)}, u32[]{:S(2)}) async-start(bf16[32,2,1024]{2,1,0:T(2,128)(2,1)} %reshape.83), calls=%async_computation.1 | async-start | bytes 262144 | tf_op jit(solution)/shard_map/all_to_all | solution.py:148
  249.6 1.5 fusion.13
  251.8 8.4 %all-to-all-done.1 = bf16[32,2,1024]{2,1,0:T(2,128)(2,1)S(1)} async-done(((bf16[32,2,1024]{2,1,0:T(2,128)(2,1)}), bf16[32,2,1024]{2,1,0:T(2,128)(2,1)S(1)}, u32[]{:S(2)}, u32[]{:S(2)}) %all-to-all-start.1) | async-done | bytes 131104 | tf_op jit(solution)/shard_map/all_to_all | solution.py:148
  260.4 2.7 %fusion.10 = bf16[64,1024]{1,0:T(8,128)(2,1)} fusion(bf16[1024,1024]{1,0:T(8,128)(2,1)} %all-gather.2.cloned.1.call-done, bf16[64,1024]{1,0:T(8,128)(2,1)S(1)} %bitcast.140, bf16[8,8,8,128]{3,2,1,0:T(8,128)(2,1)S(1)} %bitcast.135), kind=kOutput, calls=%fused_computation.24 | convolution fusion | flops 134414336 | bytes 2490368 | tf_op jit(solution)/shard_map/dot_general | solution.py:160
  (211 shorter events, 47.7 us)
Async XLA Ops:
  7.2 34.0 %copy-start = (s32[4,64]{1,0:T(4,128)S(1)}, s32[4,64]{1,0:T(4,128)}, u32[]{:S(2)}) copy-start(s32[4,64]{1,0:T(4,128)} %param.15) | copy-start | bytes 3076
  7.2 14.0 %copy-start.6 = (bf16[32,128]{1,0:T(8,128)(2,1)S(1)}, bf16[32,128]{1,0:T(8,128)(2,1)}, u32[]{:S(2)}) copy-start(bf16[32,128]{1,0:T(8,128)(2,1)} %param.21) | copy-start | bytes 24580
  7.2 26.9 %copy-start.7 = (f32[1,3,8]{2,0,1:T(1,128)S(1)}, f32[1,3,8]{2,0,1:T(1,128)}, u32[]{:S(2)}) copy-start(f32[1,3,8]{2,0,1:T(1,128)} %param.18) | copy-start | bytes 292
  7.2 33.2 %copy-start.8 = (s32[4]{0:T(128)S(1)}, s32[4]{0:T(128)}, u32[]{:S(2)}) copy-start(s32[4]{0:T(128)} %param.16) | copy-start | bytes 52
  7.2 33.9 %copy-start.5 = (bf16[2,16,1024]{2,1,0:T(8,128)(2,1)S(1)}, bf16[2,16,1024]{2,1,0:T(8,128)(2,1)}, u32[]{:S(2)}) copy-start(bf16[2,16,1024]{2,1,0:T(8,128)(2,1)} %param.17) | copy-start | bytes 196612
  9.7 32.3 %copy-start.1 = (f32[1,128,128]{2,1,0:T(8,128)S(1)}, f32[1,128,128]{2,1,0:T(8,128)}, u32[]{:S(2)}) copy-start(f32[1,128,128]{2,1,0:T(8,128)} %param.19) | copy-start | bytes 196612
  9.7 31.5 %all-to-all-start = ((bf16[32,16,384]{2,1,0:T(8,128)(2,1)}), bf16[32,16,384]{2,1,0:T(8,128)(2,1)S(1)}, u32[]{:S(2)}, u32[]{:S(2)}) async-start(bf16[32,16,384]{2,1,0:T(8,128)(2,1)} %reshape.79), calls=%async_computation | async-start | bytes 786432 | tf_op jit(solution)/shard_map/all_to_all | solution.py:78
  21.1 21.0 %copy-start.4 = (f32[1,128,128]{2,1,0:T(8,128)S(1)}, f32[1,128,128]{2,1,0:T(8,128)}, u32[]{:S(2)}) copy-start(f32[1,128,128]{2,1,0:T(8,128)} %param.20) | copy-start | bytes 196612
  21.1 239.2 %all-gather.2.cloned.1.call-start = ((), (), s32[]{:S(2)}) async-start(), calls=%async_computation.2 | async-start | bytes 2162688 | tf_op jit(solution)/shard_map/all_gather | solution.py:158
  236.3 24.1 %copy-start.3 = (bf16[4,16,1024]{2,1,0:T(8,128)(2,1)S(1)}, bf16[4,16,1024]{2,1,0:T(8,128)(2,1)}, u32[]{:S(2)}) copy-start(bf16[4,16,1024]{2,1,0:T(8,128)(2,1)} %param.13) | copy-start | bytes 393220
  239.6 20.6 %all-to-all-start.1 = ((bf16[32,2,1024]{2,1,0:T(2,128)(2,1)}), bf16[32,2,1024]{2,1,0:T(2,128)(2,1)S(1)}, u32[]{:S(2)}, u32[]{:S(2)}) async-start(bf16[32,2,1024]{2,1,0:T(2,128)(2,1)} %reshape.83), calls=%async_computation.1 | async-start | bytes 262144 | tf_op jit(solution)/shard_map/all_to_all | solution.py:148
  251.1 12.0 %copy-start.2 = (f32[128,128]{1,0:T(8,128)}, f32[128,128]{1,0:T(8,128)S(1)}, u32[]{:S(2)}) copy-start(f32[128,128]{1,0:T(8,128)S(1)} %fusion.13) | copy-start | bytes 196612
Sparse Core Ops, SparseCore 0:
  34.2 78.4 all-gather.1
where the time goes:
time: 273 us; the launch traced here: 270 us
  loops' own time  127 us (47%)
  local copies, waits for them, and re-layouts  32.4 us (12%)
  matrix products  30.3 us (11%)
  starting transfers between devices  21.3 us (8%)
  between operations  19.5 us (7%)
  other arithmetic  17.8 us (7%)
  blocking collectives  12.8 us (5%)
  waiting for transfers between devices  8.45 us (3%)
    another operation x1, loops' own time, handle(): carried = lax.fori_loop(0, block_count, visit_block, carried)  127 us
    squeeze x16, local copies, waits for them, and re-layouts, visit_block(): lax.dynamic_index_in_dim(pages_here, slot_here, 0, keepdims=False)  15.4 us
    all_gather x1, blocking collectives, shards(): wide_rows = lax.all_gather(w_out, 'gx', axis=1, tiled=True)  12.8 us
    dot_general x8, matrix products, recall(): gradient = jnp.dot(key_block.T, errors, precision=lax.Precision.HIGHEST)  12.1 us
    all_to_all x1, starting transfers between devices, shards(): lax.all_to_all(sectioned, 'gy', split_axis=0, concat_axis=1, tiled=True)  11.4 us
    lt x16, other arithmetic, visit_block(): scores = jnp.where((key_pos < length)[None, :], scores, masked_score)  11.1 us
    dynamic_slice x16, local copies, waits for them, and re-layouts, visit_block(): lax.dynamic_index_in_dim(table_row, first_page + within_block, 0, keepdim...  10.9 us
    all_to_all x1, starting transfers between devices, shards(): lax.all_to_all(for_sending(mixed), 'gy', split_axis=1, concat_axis=0, til...  9.79 us
  transfers between devices with their start and end apart: 3, of which 1 were waited for; matrix products, arithmetic and copies ran while one was open for 28% of the time, Pallas kernels for 0%

commit v1 on v0

--- a/solution.py
+++ b/solution.py
@@ -155,7 +155,10 @@
     )
     wide_rows = lax.all_gather(w_out, "gx", axis=1, tiled=True)
     flattened = tokens_here.reshape(groups * positions, D)
-    weight_piece = lax.all_gather(wide_rows, "gy", axis=0, tiled=True)
+    size = lax.axis_size("gy")
+    blocks = jnp.stack([wide_rows for _ in range(size)])
+    blocks = lax.all_to_all(blocks, "gy", split_axis=0, concat_axis=0)
+    weight_piece = jnp.concatenate(blocks, axis=0)
     taken = lax.slice_in_dim(flattened, 0, weight_piece.shape[0], axis=1)
     product = jnp.zeros((groups * positions, D), jnp.float32) + jnp.dot(
         taken, weight_piece, preferred_element_type=jnp.float32

time: 273 us -> 302 us (1.11)
  waiting for transfers between devices: 8.45 us -> 55.4 us
  between operations: 19.5 us -> 6.2 us
  loops' own time: 127 us -> 119 us
  starting transfers between devices: 21.3 us -> 26.4 us
    all_to_all x0 -> x1, waiting for transfers between devices: none -> 47.4 us  [shards(): blocks = lax.all_to_all(blocks, 'gy', split_axis=0, concat_axis=0)]
    all_to_all x0 -> x1, starting transfers between devices: none -> 9.92 us  [shards(): blocks = lax.all_to_all(blocks, 'gy', split_axis=0, concat_axis=0)]
    another operation x1, loops' own time: 127 us -> 119 us  [handle(): carried = lax.fori_loop(0, block_count, visit_block, carried)]
    all_to_all x1, waiting for transfers between devices: 8.41 us -> 0.01 us  [shards(): lax.all_to_all(for_sending(mixed), 'gy', split_axis=1, concat_axis=0, til...]
    all_to_all x1, waiting for transfers between devices: 0.01 us -> 7.97 us  [shards(): lax.all_to_all(sectioned, 'gy', split_axis=0, concat_axis=1, tiled=True)]
    all_to_all x1, starting transfers between devices: 9.79 us -> 5.13 us  [shards(): lax.all_to_all(for_sending(mixed), 'gy', split_axis=1, concat_axis=0, til...]
  transfers between devices with their start and end apart: 3 -> 3, of which waited for: 1 -> 2; matrix products, arithmetic and copies ran while one was open for 28% -> 1% of each run, Pallas kernels for 0% -> 0%
where the time goes in v1:
time: 302 us; the launch traced here: 299 us
  loops' own time  119 us (39%)
  waiting for transfers between devices  55.4 us (18%)
  local copies, waits for them, and re-layouts  33.9 us (11%)
  matrix products  30.1 us (10%)
  starting transfers between devices  26.4 us (9%)
  other arithmetic  16.4 us (5%)
  blocking collectives  11.7 us (4%)
  between operations  6.2 us (2%)
    another operation x1, loops' own time, handle(): carried = lax.fori_loop(0, block_count, visit_block, carried)  119 us
    all_to_all x1, waiting for transfers between devices, shards(): blocks = lax.all_to_all(blocks, 'gy', split_axis=0, concat_axis=0)  47.4 us
    squeeze x16, local copies, waits for them, and re-layouts, visit_block(): lax.dynamic_index_in_dim(pages_here, slot_here, 0, keepdims=False)  15.4 us
    dot_general x8, matrix products, recall(): gradient = jnp.dot(key_block.T, errors, precision=lax.Precision.HIGHEST)  12.6 us
    all_gather x1, blocking collectives, shards(): wide_rows = lax.all_gather(w_out, 'gx', axis=1, tiled=True)  11.7 us
    all_to_all x1, starting transfers between devices, shards(): lax.all_to_all(sectioned, 'gy', split_axis=0, concat_axis=1, tiled=True)  11.3 us
    dynamic_slice x16, local copies, waits for them, and re-layouts, visit_block(): lax.dynamic_index_in_dim(table_row, first_page + within_block, 0, keepdim...  10.8 us
    all_to_all x1, starting transfers between devices, shards(): blocks = lax.all_to_all(blocks, 'gy', split_axis=0, concat_axis=0)  9.92 us
  transfers between devices with their start and end apart: 3, of which 2 were waited for; matrix products, arithmetic and copies ran while one was open for 1% of the time, Pallas kernels for 0%

profile of v1, /device:TPU:8, one launch (start us, length us, event | category | flops | bytes accessed | tf_op | source)
XLA Modules:
  0.0 299.1 jit_solution(12247978605096847188)
XLA Ops:
  0.7 1.1 copy.24
  2.0 1.1 reshape.84
  3.1 11.3 %all-to-all-start = ((bf16[32,16,384]{2,1,0:T(8,128)(2,1)}), bf16[32,16,384]{2,1,0:T(8,128)(2,1)S(1)}, u32[]{:S(2)}, u32[]{:S(2)}) async-start(bf16[32,16,384]{2,1,0:T(8,128)(2,1)} %reshape.84), calls=%async_computation | async-start | bytes 786432 | tf_op jit(solution)/shard_map/all_to_all | solution.py:78
  21.0 8.0 %all-to-all-done = bf16[32,16,384]{2,1,0:T(8,128)(2,1)S(1)} async-done(((bf16[32,16,384]{2,1,0:T(8,128)(2,1)}), bf16[32,16,384]{2,1,0:T(8,128)(2,1)S(1)}, u32[]{:S(2)}, u32[]{:S(2)}) %all-to-all-start) | async-done | bytes 393248 | tf_op jit(solution)/shard_map/all_to_all | solution.py:78
  29.2 1.3 fusion.79
  31.0 170.2 %while.30 = (s32[]{:T(128)}, f32[512]{0:T(512)S(1)}, f32[512]{0:T(512)S(1)}, f32[512,128]{1,0:T(8,128)S(1)}, s32[]{:T(128)}, /*index=5*/s32[64]{0:T(128)S(1)}, b...) while((s32[]{:T(128)}, f32[512]{0:T(512)S(1)}, ...), condition=%wide.region_5.6_spmd, body=%wide.region_2.5_spmd.sunk | while | flops 137234464 | bytes 5146185 | solution.py:124
  39.7 1.0 dynamic-slice_bitcast_fusion.5
  50.4 1.0 dynamic-slice_bitcast_fusion.5
  61.0 1.0 dynamic-slice_bitcast_fusion.5
  71.6 1.0 dynamic-slice_bitcast_fusion.5
  82.3 1.0 dynamic-slice_bitcast_fusion.5
  92.9 1.0 dynamic-slice_bitcast_fusion.5
  103.6 1.0 dynamic-slice_bitcast_fusion.5
  114.2 1.0 dynamic-slice_bitcast_fusion.5
  124.8 1.0 dynamic-slice_bitcast_fusion.5
  156.8 1.0 dynamic-slice_bitcast_fusion.5
  167.4 1.0 dynamic-slice_bitcast_fusion.5
  201.7 1.6 fusion.33
  203.5 1.7 multiply_add_fusion.6
  205.4 1.6 multiply_add_fusion.5
  207.2 1.5 multiply_add_fusion.4
  208.9 1.5 multiply_add_fusion.3
  210.6 1.6 multiply_add_fusion.2
  213.7 1.6 multiply_add_fusion.1
  216.9 1.4 reduce.4
  219.0 5.1 %all-to-all-start.1 = ((bf16[32,2,1024]{2,1,0:T(2,128)(2,1)}), bf16[32,2,1024]{2,1,0:T(2,128)(2,1)S(1)}, u32[]{:S(2)}, u32[]{:S(2)}) async-start(bf16[32,2,1024]{2,1,0:T(2,128)(2,1)} %reshape.89), calls=%async_computation.1 | async-start | bytes 262144 | tf_op jit(solution)/shard_map/all_to_all | solution.py:148
  224.1 11.7 %all_gather.3 = bf16[32,1024]{1,0:T(8,128)(2,1)S(1)} all-gather(bf16[32,128]{1,0:T(8,128)(2,1)S(1)} %copy-done.7), channel_id=1, replica_groups=mesh['gx'=8,'gy'=32] {'gx'}, dimensions={1}, use_global_device_ids=true | all-gather | bytes 73728 | tf_op jit(solution)/shard_map/all_gather | solution.py:156
  235.9 1.6 stack.2
  237.4 9.9 %all-to-all-start.2 = ((bf16[32,32,1024]{2,1,0:T(8,128)(2,1)}), bf16[32,32,1024]{2,1,0:T(8,128)(2,1)S(1)}, u32[]{:S(2)}, u32[]{:S(2)}) async-start(bf16[32,32,1024]{2,1,0:T(8,128)(2,1)} %stack.2), calls=%async_computation.2 | async-start | bytes 4194304 | tf_op jit(solution)/shard_map/all_to_all | solution.py:160
  248.1 1.5 fusion.13
  250.5 47.4 %all-to-all-done.2 = bf16[32,32,1024]{2,1,0:T(8,128)(2,1)S(1)} async-done(((bf16[32,32,1024]{2,1,0:T(8,128)(2,1)}), bf16[32,32,1024]{2,1,0:T(8,128)(2,1)S(1)}, u32[]{:S(2)}, u32[]{:S(2)}) %all-to-all-start.2) | async-done | bytes 2097184 | tf_op jit(solution)/shard_map/all_to_all | solution.py:160
  297.9 1.1 fusion.10
  (213 shorter events, 49.7 us)
Async XLA Ops:
  0.6 20.4 %copy-start = (s32[4,64]{1,0:T(4,128)S(1)}, s32[4,64]{1,0:T(4,128)}, u32[]{:S(2)}) copy-start(s32[4,64]{1,0:T(4,128)} %param.15) | copy-start | bytes 3076
  0.6 13.8 %copy-start.8 = (f32[1,3,8]{2,0,1:T(1,128)S(1)}, f32[1,3,8]{2,0,1:T(1,128)}, u32[]{:S(2)}) copy-start(f32[1,3,8]{2,0,1:T(1,128)} %param.18) | copy-start | bytes 292
  0.7 19.7 %copy-start.9 = (s32[4]{0:T(128)S(1)}, s32[4]{0:T(128)}, u32[]{:S(2)}) copy-start(s32[4]{0:T(128)} %param.16) | copy-start | bytes 52
  0.7 20.3 %copy-start.6 = (bf16[2,16,1024]{2,1,0:T(8,128)(2,1)S(1)}, bf16[2,16,1024]{2,1,0:T(8,128)(2,1)}, u32[]{:S(2)}) copy-start(bf16[2,16,1024]{2,1,0:T(8,128)(2,1)} %param.17) | copy-start | bytes 196612
  3.1 25.9 %all-to-all-start = ((bf16[32,16,384]{2,1,0:T(8,128)(2,1)}), bf16[32,16,384]{2,1,0:T(8,128)(2,1)S(1)}, u32[]{:S(2)}, u32[]{:S(2)}) async-start(bf16[32,16,384]{2,1,0:T(8,128)(2,1)} %reshape.84), calls=%async_computation | async-start | bytes 786432 | tf_op jit(solution)/shard_map/all_to_all | solution.py:78
  31.0 170.5 %copy-start.2 = (f32[1,128,128]{2,1,0:T(8,128)S(1)}, f32[1,128,128]{2,1,0:T(8,128)}, u32[]{:S(2)}) copy-start(f32[1,128,128]{2,1,0:T(8,128)} %param.19) | copy-start | bytes 196612
  31.0 170.7 %copy-start.5 = (f32[1,128,128]{2,1,0:T(8,128)S(1)}, f32[1,128,128]{2,1,0:T(8,128)}, u32[]{:S(2)}) copy-start(f32[1,128,128]{2,1,0:T(8,128)} %param.20) | copy-start | bytes 196612
  203.3 12.2 %copy-start.1 = (f32[512,512]{0,1:T(8,128)S(1)}, f32[512,512]{0,1:T(8,128)}, u32[]{:S(2)}) copy-start(f32[512,512]{0,1:T(8,128)} %get-tuple-element.338) | copy-start | bytes 3145732
  215.5 8.6 %copy-start.7 = (bf16[32,128]{1,0:T(8,128)(2,1)S(1)}, bf16[32,128]{1,0:T(8,128)(2,1)}, u32[]{:S(2)}) copy-start(bf16[32,128]{1,0:T(8,128)(2,1)} %param.21) | copy-start | bytes 24580
  219.0 16.9 %all-to-all-start.1 = ((bf16[32,2,1024]{2,1,0:T(2,128)(2,1)}), bf16[32,2,1024]{2,1,0:T(2,128)(2,1)S(1)}, u32[]{:S(2)}, u32[]{:S(2)}) async-start(bf16[32,2,1024]{2,1,0:T(2,128)(2,1)} %reshape.89), calls=%async_computation.1 | async-start | bytes 262144 | tf_op jit(solution)/shard_map/all_to_all | solution.py:148
  237.4 60.5 %copy-start.4 = (bf16[4,16,1024]{2,1,0:T(8,128)(2,1)S(1)}, bf16[4,16,1024]{2,1,0:T(8,128)(2,1)}, u32[]{:S(2)}) copy-start(bf16[4,16,1024]{2,1,0:T(8,128)(2,1)} %param.13) | copy-start | bytes 393220
  237.4 60.5 %all-to-all-start.2 = ((bf16[32,32,1024]{2,1,0:T(8,128)(2,1)}), bf16[32,32,1024]{2,1,0:T(8,128)(2,1)S(1)}, u32[]{:S(2)}, u32[]{:S(2)}) async-start(bf16[32,32,1024]{2,1,0:T(8,128)(2,1)} %stack.2), calls=%async_computation.2 | async-start | bytes 4194304 | tf_op jit(solution)/shard_map/all_to_all | solution.py:160
  249.6 49.4 %copy-start.3 = (f32[128,128]{1,0:T(8,128)}, f32[128,128]{1,0:T(8,128)S(1)}, u32[]{:S(2)}) copy-start(f32[128,128]{1,0:T(8,128)S(1)} %fusion.13) | copy-start | bytes 196612
